TPU v7x, 32 devices: a whole 2x2x4 slice. The times are simulated.
32 devices in a mesh: row: 8 (over y, x, core), col: 4 (over z).
Axes of the slice: x: 2, y: 2, z: 4, core: 2. Of those that a mesh axis runs over, the one named last changes fastest.
Arguments:
- design: bfloat16 [512, 90112], P(('row', 'col')), may hold values from -6 to 6
- arc_partials: float32 [32, 6, 16], P(('row', 'col')), may hold values from -6 to 6
- arc_id: int32 [32], P(('row', 'col')), may hold values from 0 to 7
- arc_weight: float32 [8], replicated, may hold values from 0.25 to 4
Outputs:
- normal_slab: float32 [90112, 2048], P('row', 'col')
All inputs are finite; a program needn't handle non-finite values.
Results may differ from a plain program's by a relative error of at most 0.0003.
The roundings to bfloat16 on the way count: a program that leaves them out, or rounds other values in their place, can miss the bound.
Values may be sent and summed in bfloat16 or wider, within the bound.
A program may use at most 128 MiB of HBM per device.

v0:
```python
import jax
import jax.numpy as jnp
from jax import lax
from jax.sharding import PartitionSpec as P

SLAB = 2048


ridge = 4.0


def solve_small(matrix, rhs):
    order = matrix.shape[-1]
    for pivot in range(order):
        scale = 1.0 / matrix[..., pivot, pivot]
        row_mat = matrix[..., pivot, :] * scale[..., None]
        row_rhs = rhs[..., pivot, :] * scale[..., None]
        factor = matrix[..., :, pivot]
        matrix = matrix - factor[..., :, None] * row_mat[..., None, :]
        rhs = rhs - factor[..., :, None] * row_rhs[..., None, :]
        matrix = matrix.at[..., pivot, :].set(row_mat)
        rhs = rhs.at[..., pivot, :].set(row_rhs)
    return rhs


def own_reduced(design, arc_partials, arc_id, arc_weight):
    high = lax.Precision.HIGHEST
    slab_rows = design[:, :SLAB].astype(jnp.float32)
    partials = arc_partials[0]
    coupling = jnp.dot(partials, slab_rows, precision=high, preferred_element_type=jnp.float32)
    gram = jnp.dot(partials, partials.T, precision=high, preferred_element_type=jnp.float32)
    arc_count = arc_weight.shape[0]
    select = (jnp.arange(arc_count) == arc_id[0]).astype(jnp.float32)
    arc_gram, arc_coupling = lax.psum(
        (select[:, None, None] * gram[None], select[:, None, None] * coupling[None]), ("row", "col")
    )
    order = partials.shape[0]
    own_gram = jnp.sum(select[:, None, None] * arc_gram, axis=0) + ridge * jnp.eye(
        order, dtype=jnp.float32
    )
    own_coupling = jnp.sum(select[:, None, None] * arc_coupling, axis=0)
    solved = solve_small(own_gram, own_coupling)
    reduced = slab_rows - jnp.dot(
        partials.T, solved, precision=high, preferred_element_type=jnp.float32
    )
    weight = jnp.sum(select * arc_weight)
    return (weight * reduced).astype(jnp.bfloat16)


def make_accumulate(ordered, piece):
    return lax.dot_general(
        piece, ordered, (((0,), (0,)), ((), ())), preferred_element_type=jnp.float32
    )


def col_major(slab_global, row_count, col_count, rows_dev):
    width = slab_global.shape[1]
    ordered = slab_global.reshape(row_count, col_count, rows_dev, width)
    return ordered.transpose(1, 0, 2, 3).reshape(rows_dev * row_count * col_count, width)


def local(design, arc_partials, arc_id, arc_weight):
    rows_dev = design.shape[0]
    row_count = lax.axis_size("row")
    col_count = lax.axis_size("col")
    devices = row_count * col_count
    epochs = rows_dev * devices
    eliminated_own = own_reduced(design, arc_partials, arc_id, arc_weight)
    regrouped = lax.all_to_all(design, "row", split_axis=1, concat_axis=0, tiled=True)
    columns = lax.all_to_all(eliminated_own, "col", split_axis=1, concat_axis=0, tiled=True)
    slab_global = lax.all_gather(columns, "row", axis=0, tiled=True)
    ordered = col_major(slab_global, row_count, col_count, rows_dev)
    normal = make_accumulate(ordered, lax.all_gather(regrouped, "col", axis=0, tiled=True))
    return normal * (1.0 / epochs)


def solution(mesh):
    placed = (P(("row", "col"), None), P(("row", "col"), None, None), P(("row", "col")), P())
    return jax.shard_map(
        local, mesh=mesh, in_specs=placed, out_specs=P("row", "col"), check_vma=False
    )
```

profile of v0, /device:TPU:0, one launch (start us, length us, event | category | flops | bytes accessed | tf_op | source)
XLA Modules:
  0.0 400.1 jit_solution(14108734418693655313)
XLA Ops:
  7.4 3.6 copy.42
  11.0 5.2 %all-to-all-start.1 = ((bf16[16,8,11264]{2,0,1:T(8,128)(2,1)}), bf16[16,8,11264]{2,0,1:T(8,128)(2,1)S(1)}, u32[]{:S(2)}, u32[]{:S(2)}) async-start(bf16[16,8,11264]{2,0,1:T(8,128)(2,1)} %bitcast.64), calls=%async_computation.1 | async-start | bytes 5767168 | tf_op jit(solution)/shard_map/all_to_all | solution.py:69
  16.9 1.0 fusion.3
  17.9 0.8 broadcast_multiply_fusion
  18.8 33.2 %all-to-all-done.1 = bf16[16,8,11264]{2,0,1:T(8,128)(2,1)S(1)} async-done(((bf16[16,8,11264]{2,0,1:T(8,128)(2,1)}), bf16[16,8,11264]{2,0,1:T(8,128)(2,1)S(1)}, u32[]{:S(2)}, u32[]{:S(2)}) %all-to-all-start.1) | async-done | bytes 2883616 | tf_op jit(solution)/shard_map/all_to_all | solution.py:69
  52.0 1.6 copy-done
  53.8 50.2 %psum.15 = f32[8,6,6]{2,0,1:T(8,128)S(1)} all-reduce(f32[8,6,6]{2,0,1:T(8,128)S(1)} %broadcast_multiply_fusion.1), channel_id=1, replica_groups=mesh['row'=8,'col'=4] {'row','col'}, use_global_device_ids=true, to_apply=%region_3.0 | all-reduce | flops 288 | bytes 2304 | tf_op jit(solution)/shard_map/psum | solution.py:34
  104.1 0.5 slice.240
  105.5 0.6 slice.244
  106.8 0.2 slice_reduce_fusion.4
  107.1 0.6 slice.248
  108.4 0.2 slice_reduce_fusion.3
  108.7 0.6 slice.252
  110.0 0.2 slice_reduce_fusion.2
  110.3 0.6 slice.256
  111.5 0.2 slice_reduce_fusion.1
  111.8 0.6 slice.260
  113.2 0.6 fusion.12
  113.8 0.2 slice_reduce_fusion
  114.0 216.3 %all-reduce.2.cloned.1.call-done = f32[8,6,2048]{2,0,1:T(8,128)} async-done(((f32[8,6,2048]{2,0,1:T(8,128)}), f32[8,6,2048]{2,0,1:T(8,128)}) %all-reduce.2.cloned.1.call-update) | async-done | bytes 393232 | tf_op jit(solution)/shard_map/psum | solution.py:34
  330.3 1.2 multiply_reduce_fusion
  331.6 0.2 scatter.36
  331.9 0.2 scatter.40
  332.1 0.2 scatter.44
  332.4 0.2 scatter.46
  332.7 0.2 scatter.50
  333.0 0.2 scatter.54
  333.2 1.7 fusion.2
  334.9 9.2 %all_to_all.38 = bf16[16,4,512]{2,0,1:T(8,128)(2,1)S(1)} all-to-all(bf16[16,4,512]{2,0,1:T(8,128)(2,1)S(1)} %bitcast.70), channel_id=1, replica_groups=mesh['row'=8,'col'=4] {'col'}, dimensions={1} | all-to-all | bytes 131072 | tf_op jit(solution)/shard_map/all_to_all | solution.py:70
  344.1 9.8 %all_gather.6 = bf16[512,512]{1,0:T(8,128)(2,1)S(1)} all-gather(bf16[64,512]{1,0:T(8,128)(2,1)S(1)} %bitcast.69), channel_id=1, replica_groups=mesh['row'=8,'col'=4] {'row'}, dimensions={0}, use_global_device_ids=true | all-gather | bytes 589824 | tf_op jit(solution)/shard_map/all_gather | solution.py:71
  354.0 15.2 %multiply_bitcast_fusion = f32[11264,512]{0,1:T(8,128)} fusion(bf16[512,512]{1,0:T(8,128)(2,1)S(1)} %bitcast.65, bf16[512,11264]{1,0:T(8,128)(2,1)} %all-gather.2.cloned.1.call-done), kind=kOutput, calls=%fused_computation | convolution fusion | flops 5911347200 | bytes 35127296 | tf_op jit(solution)/shard_map/dot_general | solution.py:51
  369.1 23.5 %copy.24 = f32[11264,512]{1,0:T(8,128)} copy(f32[11264,512]{0,1:T(8,128)} %multiply_bitcast_fusion) | data formatting | bytes 46137344 | tf_op jit(solution)/shard_map/mul | solution.py:74
  (50 shorter events, 1.7 us)
Async XLA Ops:
  7.4 9.5 %copy-start.1 = (f32[1,6,16]{2,0,1:T(1,128)S(1)}, f32[1,6,16]{2,0,1:T(1,128)}, u32[]{:S(2)}) copy-start(f32[1,6,16]{2,0,1:T(1,128)} %param.27) | copy-start | bytes 1156
  7.4 105.8 %copy-start.2 = (f32[8]{0:T(128)S(1)}, f32[8]{0:T(128)}, u32[]{:S(2)}) copy-start(f32[8]{0:T(128)} %param.29) | copy-start | bytes 100
  11.0 41.0 %all-to-all-start.1 = ((bf16[16,8,11264]{2,0,1:T(8,128)(2,1)}), bf16[16,8,11264]{2,0,1:T(8,128)(2,1)S(1)}, u32[]{:S(2)}, u32[]{:S(2)}) async-start(bf16[16,8,11264]{2,0,1:T(8,128)(2,1)} %bitcast.64), calls=%async_computation.1 | async-start | bytes 5767168 | tf_op jit(solution)/shard_map/all_to_all | solution.py:69
  16.2 314.1 %all-reduce.2.cloned.1.call-start = ((), (), s32[]{:S(2)}) async-start(), calls=%async_computation.2 | async-start | bytes 786432 | tf_op jit(solution)/shard_map/psum | solution.py:34
  18.8 335.2 %all-gather.2.cloned.1.call-start = ((), (), s32[]{:S(2)}) async-start(), calls=%async_computation.3 | async-start | bytes 14417920 | tf_op jit(solution)/shard_map/all_gather | solution.py:73
  52.0 1.6 copy-start
Sparse Core Ops, SparseCore 0:
  22.3 307.9 all-reduce.1
Sparse Core Ops, SparseCore 1:
  53.7 201.6 all-gather.1
where the time goes:
time: 401 us; the launch traced here: 400 us
  waiting for transfers between devices  250 us (62%)
  blocking collectives  69.1 us (17%)
  local copies, waits for them, and re-layouts  34.6 us (9%)
  between operations  19.7 us (5%)
  matrix products  18 us (4%)
  starting transfers between devices  5.28 us (1%)
    psum x1, waiting for transfers between devices, own_reduced(): lax.psum((select[:, None, None] * gram[None], select[:, None, None] * cou...  216 us
    psum x1, blocking collectives, own_reduced(): lax.psum((select[:, None, None] * gram[None], select[:, None, None] * cou...  50.2 us
    all_to_all x1, waiting for transfers between devices, local(): lax.all_to_all(design, 'row', split_axis=1, concat_axis=0, tiled=True)  33.2 us
    mul x1, local copies, waits for them, and re-layouts, local(): return normal * (1.0 / epochs)  23.5 us
    dot_general x1, matrix products, make_accumulate(): lax.dot_general(piece, ordered, (((0,), (0,)), ((), ())), preferred_eleme...  15.2 us
    all_gather x1, blocking collectives, local(): slab_global = lax.all_gather(columns, 'row', axis=0, tiled=True)  9.79 us
    all_to_all x1, blocking collectives, local(): lax.all_to_all(eliminated_own, 'col', split_axis=1, concat_axis=0, tiled=...  9.18 us
  transfers between devices with their start and end apart: 3, of which 2 were waited for; matrix products, arithmetic and copies ran while one was open for 3% of the time, Pallas kernels for 0%

commit v1 on v0

v1 whole, which is shorter than its diff:
```python
import functools

import jax
import jax.numpy as jnp
from jax import lax
from jax.experimental import pallas as pl
from jax.experimental.pallas import tpu as pltpu
from jax.sharding import PartitionSpec as P

SLAB = 2048
SHARES = (4, 12, 6)


ridge = 4.0


def solve_small(matrix, rhs):
    order = matrix.shape[-1]
    for pivot in range(order):
        scale = 1.0 / matrix[..., pivot, pivot]
        row_mat = matrix[..., pivot, :] * scale[..., None]
        row_rhs = rhs[..., pivot, :] * scale[..., None]
        factor = matrix[..., :, pivot]
        matrix = matrix - factor[..., :, None] * row_mat[..., None, :]
        rhs = rhs - factor[..., :, None] * row_rhs[..., None, :]
        matrix = matrix.at[..., pivot, :].set(row_mat)
        rhs = rhs.at[..., pivot, :].set(row_rhs)
    return rhs


def after(value, token):
    return lax.optimization_barrier((value, token))[0]


def eliminated_columns(slab, partials, ids, arc_weight):
    high = lax.Precision.HIGHEST
    segments, order, rows_dev = partials.shape
    arcs = arc_weight.shape[0]
    select = (jnp.arange(arcs)[:, None] == ids[None, :]).astype(jnp.float32)
    gram = jnp.einsum("npe,nqe->npq", partials, partials, precision=high)
    arc_gram = jnp.einsum("an,npq->apq", select, gram, precision=high)
    arc_gram = arc_gram + ridge * jnp.eye(order, dtype=jnp.float32)
    spread = select[:, None, :, None] * partials.transpose(1, 0, 2)[None]
    spread = spread.reshape(arcs * order, segments * rows_dev)
    values = slab.astype(jnp.float32)
    coupling = jnp.dot(spread, values, precision=high, preferred_element_type=jnp.float32)
    solved = solve_small(arc_gram, coupling.reshape(arcs, order, -1))
    fitted = lax.dot_general(
        spread,
        solved.reshape(arcs * order, -1),
        (((0,), (0,)), ((), ())),
        precision=high,
        preferred_element_type=jnp.float32,
    )
    weights = jnp.repeat(jnp.sum(select * arc_weight[:, None], axis=0), rows_dev)
    return (weights[:, None] * (values - fitted)).astype(jnp.bfloat16)


def product_kernel(scale, piece_ref, slab_ref, *rest):
    out_ref = rest[-1]
    out_ref[...] = scale * lax.dot_general(
        piece_ref[...],
        slab_ref[...],
        (((0,), (0,)), ((), ())),
        preferred_element_type=jnp.float32,
    )


def product_into(total, piece, ordered, first, tile, rows, scale):
    epochs, width = piece.shape
    columns = ordered.shape[1]
    operands = [piece, ordered]
    in_specs = [
        pl.BlockSpec((epochs, tile), lambda i: (0, i)),
        pl.BlockSpec((epochs, columns), lambda i: (0, 0)),
    ]
    aliases = {}
    if total is not None:
        operands.append(total)
        in_specs.append(pl.BlockSpec(memory_space=pl.ANY))
        aliases = {2: 0}
    return pl.pallas_call(
        functools.partial(product_kernel, scale),
        out_shape=jax.ShapeDtypeStruct((rows, columns), jnp.float32),
        grid=(width // tile,),
        in_specs=in_specs,
        out_specs=pl.BlockSpec((tile, columns), lambda i: (first // tile + i, 0)),
        input_output_aliases=aliases,
        compiler_params=pltpu.CompilerParams(vmem_limit_bytes=40 << 20),
        cost_estimate=pl.CostEstimate(
            flops=2 * epochs * width * columns,
            bytes_accessed=2 * epochs * (width + columns) + 4 * width * columns,
            transcendentals=0,
        ),
    )(*operands)


def cuts(rows):
    tile = next(t for t in (512, 256, 128) if rows % t == 0)
    tiles, ends, seen = rows // tile, [], 0
    for share in SHARES:
        seen += share
        ends.append(tiles * seen // sum(SHARES) * tile)
    starts = [0] + ends[:-1]
    return tile, [(a, b - a) for a, b in zip(starts, ends) if b > a]


def local(design, arc_partials, arc_id, arc_weight):
    rows_dev, coefficients = design.shape
    row_count = lax.axis_size("row")
    col_count = lax.axis_size("col")
    devices = row_count * col_count
    epochs = rows_dev * devices
    rows = coefficients // row_count
    order = arc_partials.shape[1]
    tile, pieces = cuts(rows)
    split = design.reshape(rows_dev, row_count, rows)

    gathered, token = [], None
    ordered = None
    for number, (first, width) in enumerate(pieces):
        source = split[:, :, first : first + width]
        if token is not None:
            source = after(source, token)
        source = source.transpose(1, 0, 2)
        own = lax.all_to_all(source, "row", split_axis=0, concat_axis=0, tiled=True)
        token = own
        gathered.append(
            lax.all_gather(own.reshape(row_count * rows_dev, width), "col", axis=0, tiled=True)
        )
        if number == 1:
            slab_own = after(design[:, :SLAB], token)
            columns = lax.all_to_all(slab_own, "col", split_axis=1, concat_axis=0, tiled=True)
            facts = jnp.concatenate(
                [arc_partials.reshape(1, -1), arc_id.astype(jnp.float32)[:, None]], axis=1
            )
            width_facts = facts.shape[1]
            facts = jnp.broadcast_to(after(facts, columns), (devices, width_facts))
            facts = lax.all_to_all(facts, ("row", "col"), split_axis=0, concat_axis=0, tiled=True)
            spread = jnp.broadcast_to(
                after(columns, facts)[None], (row_count,) + columns.shape
            )
            slab = lax.all_to_all(spread, "row", split_axis=0, concat_axis=0, tiled=True)
            token = slab
            slab = slab.reshape(epochs, columns.shape[1])
            partials = facts[:, :-1].reshape(devices, order, rows_dev)
            ids = facts[:, -1].astype(jnp.int32)
            eliminated = eliminated_columns(slab, partials, ids, arc_weight)
            ordered = eliminated.reshape(row_count, col_count, rows_dev, -1)
            ordered = ordered.transpose(1, 0, 2, 3).reshape(epochs, -1)

    total = None
    for (first, width), piece in zip(pieces, gathered):
        total = product_into(total, piece, ordered, first, tile, rows, 1.0 / epochs)
    return total


def solution(mesh):
    placed = (P(("row", "col"), None), P(("row", "col"), None, None), P(("row", "col")), P())
    return jax.shard_map(
        local, mesh=mesh, in_specs=placed, out_specs=P("row", "col"), check_vma=False
    )
```

time: 401 us -> 265 us (0.66)
  waiting for transfers between devices: 250 us -> 157 us
  blocking collectives: 69.1 us -> 38.9 us
  Pallas kernels: 0 us -> 17.9 us
  local copies, waits for them, and re-layouts: 34.6 us -> 17.6 us
  matrix products: 18 us -> 2.04 us
  starting transfers between devices: 5.28 us -> 14.6 us
  between operations: 19.7 us -> 14.2 us
    psum x1 -> x0, waiting for transfers between devices: 216 us -> none  [own_reduced(): lax.psum((select[:, None, None] * gram[None], select[:, None, None] * cou...]
    all_gather x1 -> x3, waiting for transfers between devices: 0.03 us -> 123 us  [local(): lax.all_gather(own.reshape(row_count * rows_dev, width), 'col', axis=0, t...]
    psum x1 -> x0, blocking collectives: 50.2 us -> none  [own_reduced(): lax.psum((select[:, None, None] * gram[None], select[:, None, None] * cou...]
    all_to_all x1 -> x2, blocking collectives: 9.18 us -> 38.9 us  [local(): own = lax.all_to_all(source, 'row', split_axis=0, concat_axis=0, tiled=True)]
    mul x1 -> x11, local copies, waits for them, and re-layouts: 23.5 us -> 0.81 us  [the longest x4 0.71 us: eliminated_columns(): spread = select[:, None, :, None] * partials.transpose(1, 0, 2)[None]]
    pallas_call x0 -> x3, Pallas kernels: none -> 17.9 us  [product_into(): pl.pallas_call(functools.partial(product_kernel, scale), out_shape=jax.Sh...]
    dot_general x4, matrix products: 18 us -> 2.04 us  [the longest x1 1.06 us: eliminated_columns(): lax.dot_general(spread, solved.reshape(arcs * order, -1), (((0,), (0,)),...]
    all_gather x1 -> x0, blocking collectives: 9.79 us -> none  [local(): slab_global = lax.all_gather(columns, 'row', axis=0, tiled=True)]
  transfers between devices with their start and end apart: 3 -> 7, of which waited for: 2 -> 6; matrix products, arithmetic and copies ran while one was open for 3% -> 4% of each run, Pallas kernels for 0% -> 5%
where the time goes in v1:
time: 265 us; the launch traced here: 264 us
  waiting for transfers between devices  157 us (59%)
  blocking collectives  38.9 us (15%)
  Pallas kernels  17.9 us (7%)
  local copies, waits for them, and re-layouts  17.6 us (7%)
  starting transfers between devices  14.6 us (6%)
  between operations  14.2 us (5%)
    all_gather x3, waiting for transfers between devices, local(): lax.all_gather(own.reshape(row_count * rows_dev, width), 'col', axis=0, t...  123 us
    all_to_all x2, blocking collectives, local(): own = lax.all_to_all(source, 'row', split_axis=0, concat_axis=0, tiled=True)  38.9 us
    pallas_call x3, Pallas kernels, product_into(): pl.pallas_call(functools.partial(product_kernel, scale), out_shape=jax.Sh...  17.9 us
    all_to_all x1, waiting for transfers between devices, local(): own = lax.all_to_all(source, 'row', split_axis=0, concat_axis=0, tiled=True)  11.5 us
    unnamed x14, local copies, waits for them, and re-layouts  10.8 us
    all_to_all x1, waiting for transfers between devices, local(): lax.all_to_all(spread, 'row', split_axis=0, concat_axis=0, tiled=True)  8.83 us
    all_to_all x1, waiting for transfers between devices, local(): lax.all_to_all(slab_own, 'col', split_axis=1, concat_axis=0, tiled=True)  7.64 us
    all_to_all x1, waiting for transfers between devices, local(): lax.all_to_all(facts, ('row', 'col'), split_axis=0, concat_axis=0, tiled=...  5.8 us
  transfers between devices with their start and end apart: 7, of which 6 were waited for; matrix products, arithmetic and copies ran while one was open for 4% of the time, Pallas kernels for 5%

profile of v1, /device:TPU:0, one launch (start us, length us, event | category | flops | bytes accessed | tf_op | source)
XLA Modules:
  0.0 264.1 jit_solution(758127962315767038)
XLA Ops:
  6.5 3.4 %copy.168 = bf16[2,8,8,11264]{3,2,1,0:T(8,128)(2,1)S(1)} copy(bf16[2,8,8,11264]{3,1,2,0:T(8,128)(2,1)} %bitcast.116) | data formatting | bytes 5767168
  10.0 0.3 copy.179
  10.3 14.8 %all_to_all.48 = bf16[8,16,2048]{2,1,0:T(8,128)(2,1)} all-to-all(bf16[8,16,2048]{2,1,0:T(8,128)(2,1)S(1)} %bitcast.119), channel_id=1, replica_groups=mesh['row'=8,'col'=4] {'row'}, dimensions={0} | all-to-all | bytes 1048576 | tf_op jit(solution)/shard_map/all_to_all | solution.py:126
  25.3 0.9 copy.165
  26.2 24.1 %all_to_all.49 = bf16[8,16,6144]{2,1,0:T(8,128)(2,1)} all-to-all(bf16[8,16,6144]{2,1,0:T(8,128)(2,1)S(1)} %bitcast.112), channel_id=1, replica_groups=mesh['row'=8,'col'=4] {'row'}, dimensions={0} | all-to-all | bytes 3145728 | tf_op jit(solution)/shard_map/all_to_all | solution.py:126
  50.3 0.8 slice.308
  51.9 0.6 copy.180
  52.5 4.9 %all-to-all-start.2 = ((bf16[16,4,512]{2,0,1:T(8,128)(2,1)}), bf16[16,4,512]{2,0,1:T(8,128)(2,1)S(1)}, u32[]{:S(2)}, u32[]{:S(2)}) async-start(bf16[16,4,512]{2,0,1:T(8,128)(2,1)} %bitcast.98), calls=%async_computation.2 | async-start | bytes 131072 | tf_op jit(solution)/shard_map/all_to_all | solution.py:133
  57.5 7.6 %all-to-all-done.2 = bf16[16,4,512]{2,0,1:T(8,128)(2,1)S(1)} async-done(((bf16[16,4,512]{2,0,1:T(8,128)(2,1)}), bf16[16,4,512]{2,0,1:T(8,128)(2,1)S(1)}, u32[]{:S(2)}, u32[]{:S(2)}) %all-to-all-start.2) | async-done | bytes 65568 | tf_op jit(solution)/shard_map/all_to_all | solution.py:133
  65.1 0.6 broadcast_in_dim.9
  65.7 2.5 all-to-all-start.3
  68.3 1.3 copy.164
  69.7 5.8 %all-to-all-done.3 = f32[32,1,97]{2,1,0:T(1,128)S(1)} async-done(((f32[32,1,97]{2,1,0:T(1,128)}), f32[32,1,97]{2,1,0:T(1,128)S(1)}, u32[]{:S(2)}, u32[]{:S(2)}) %all-to-all-start.3) | async-done | bytes 12448 | tf_op jit(solution)/shard_map/all_to_all | solution.py:139
  75.7 0.4 fusion.41
  76.1 0.2 convolution_add_fusion
  76.6 0.8 broadcast_in_dim.10
  77.4 3.5 %all-to-all-start.4 = ((bf16[8,64,512]{2,1,0:T(8,128)(2,1)}), bf16[8,64,512]{2,1,0:T(8,128)(2,1)S(1)}, u32[]{:S(2)}, u32[]{:S(2)}) async-start(bf16[8,64,512]{2,1,0:T(8,128)(2,1)} %broadcast_in_dim.10), calls=%async_computation.4 | async-start | bytes 1048576 | tf_op jit(solution)/shard_map/all_to_all | solution.py:143
  81.7 8.8 %all-to-all-done.4 = bf16[8,64,512]{2,1,0:T(8,128)(2,1)S(1)} async-done(((bf16[8,64,512]{2,1,0:T(8,128)(2,1)}), bf16[8,64,512]{2,1,0:T(8,128)(2,1)S(1)}, u32[]{:S(2)}, u32[]{:S(2)}) %all-to-all-start.4) | async-done | bytes 524320 | tf_op jit(solution)/shard_map/all_to_all | solution.py:143
  90.6 3.5 %all-to-all-start.5 = ((bf16[8,16,3072]{2,1,0:T(8,128)(2,1)}), bf16[8,16,3072]{2,1,0:T(8,128)(2,1)S(1)}, u32[]{:S(2)}, u32[]{:S(2)}) async-start(bf16[8,16,3072]{2,1,0:T(8,128)(2,1)} %bitcast.8), calls=%async_computation.5 | async-start | bytes 1572864 | tf_op jit(solution)/shard_map/all_to_all | solution.py:126
  94.3 0.4 mul.356
  94.7 0.4 fusion.3
  95.1 11.5 %all-to-all-done.5 = bf16[8,16,3072]{2,1,0:T(8,128)(2,1)S(1)} async-done(((bf16[8,16,3072]{2,1,0:T(8,128)(2,1)}), bf16[8,16,3072]{2,1,0:T(8,128)(2,1)S(1)}, u32[]{:S(2)}, u32[]{:S(2)}) %all-to-all-start.5) | async-done | bytes 786464 | tf_op jit(solution)/shard_map/all_to_all | solution.py:126
  106.6 0.9 copy-done.3
  109.0 1.1 fusion.1
  110.1 1.6 copy-done.2
  111.7 3.5 %shard_map.46.rest_0_ = f32[11264,512]{1,0:T(8,128)} custom-call(bf16[512,2048]{1,0:T(8,128)(2,1)S(1)} %copy-done.2, bf16[512,512]{1,0:T(8,128)(2,1)S(1)} %bitcast.105), custom_call_target="tpu_custom_call" | custom-call | flops 1073741824 | bytes 6815744 | tf_op jit(solution)/shard_map/pallas_call | solution.py:82
  115.2 72.1 %all-gather.6.cloned.1.call-done.piece_ref = bf16[512,6144]{1,0:T(8,128)(2,1)} async-done(((bf16[128,6144]{1,0:T(8,128)(2,1)}), bf16[512,6144]{1,0:T(8,128)(2,1)}) %all-gather.6.cloned.1.call-update) | async-done | bytes 6291472 | tf_op jit(solution)/shard_map/all_gather | solution.py:129
  187.3 2.8 %copy-done = bf16[512,6144]{1,0:T(8,128)(2,1)S(1)} copy-done((bf16[512,6144]{1,0:T(8,128)(2,1)S(1)}, bf16[512,6144]{1,0:T(8,128)(2,1)}, u32[]{:S(2)}) %copy-start) | copy-done | bytes 6291480
  190.1 9.4 %shard_map.47.rest_0_ = f32[11264,512]{1,0:T(8,128)} custom-call(bf16[512,6144]{1,0:T(8,128)(2,1)S(1)} %copy-done, bf16[512,512]{1,0:T(8,128)(2,1)S(1)} %bitcast.106, f32[11264,512]{1,0:T(8,128)} %shard_map.46.rest_0_), custom_call_target="tpu_custom_call", output_to_operand_aliasing={{}: (2, {})} | custom-call | flops 3221225472 | bytes 19398656 | tf_op jit(solution)/shard_map/pallas_call | solution.py:82
  199.5 51.2 %all-gather.4.cloned.1.call-done.piece_ref = bf16[512,3072]{1,0:T(8,128)(2,1)} async-done(((bf16[128,3072]{1,0:T(8,128)(2,1)}), bf16[512,3072]{1,0:T(8,128)(2,1)}) %all-gather.4.cloned.1.call-update) | async-done | bytes 3145744 | tf_op jit(solution)/shard_map/all_gather | solution.py:129
  250.7 1.9 copy-done.1
  252.6 5.0 %shard_map.48 = f32[11264,512]{1,0:T(8,128)} custom-call(bf16[512,3072]{1,0:T(8,128)(2,1)S(1)} %copy-done.1, bf16[512,512]{1,0:T(8,128)(2,1)S(1)} %bitcast.107, f32[11264,512]{1,0:T(8,128)} %shard_map.47.rest_0_), custom_call_target="tpu_custom_call", output_to_operand_aliasing={{}: (2, {})} | custom-call | flops 1610612736 | bytes 9961472 | tf_op jit(solution)/shard_map/pallas_call | solution.py:82
  (89 shorter events, 3.2 us)
Async XLA Ops:
  6.5 103.6 %all-gather.8.cloned.1.call-start = ((), (), s32[]{:S(2)}) async-start(), calls=%async_computation.8 | async-start | bytes 2621440 | tf_op jit(solution)/shard_map/all_gather | solution.py:129
  25.1 162.2 %all-gather.6.cloned.1.call-start = ((), (), s32[]{:S(2)}) async-start(), calls=%async_computation.7 | async-start | bytes 7864320 | tf_op jit(solution)/shard_map/all_gather | solution.py:129
  26.2 25.6 %copy-start.4 = (f32[1,6,16]{2,0,1:T(1,128)S(1)}, f32[1,6,16]{2,0,1:T(1,128)}, u32[]{:S(2)}) copy-start(f32[1,6,16]{2,0,1:T(1,128)} %param.27) | copy-start | bytes 1156
  52.5 12.6 %all-to-all-start.2 = ((bf16[16,4,512]{2,0,1:T(8,128)(2,1)}), bf16[16,4,512]{2,0,1:T(8,128)(2,1)S(1)}, u32[]{:S(2)}, u32[]{:S(2)}) async-start(bf16[16,4,512]{2,0,1:T(8,128)(2,1)} %bitcast.98), calls=%async_computation.2 | async-start | bytes 131072 | tf_op jit(solution)/shard_map/all_to_all | solution.py:133
  65.7 9.8 %all-to-all-start.3 = ((f32[32,1,97]{2,1,0:T(1,128)}), f32[32,1,97]{2,1,0:T(1,128)S(1)}, u32[]{:S(2)}, u32[]{:S(2)}) async-start(f32[32,1,97]{2,1,0:T(1,128)} %broadcast_in_dim.9), calls=%async_computation.3 | async-start | bytes 32768 | tf_op jit(solution)/shard_map/all_to_all | solution.py:139
  68.3 12.7 %copy-start.5 = (f32[8]{0:T(128)S(1)}, f32[8]{0:T(128)}, u32[]{:S(2)}) copy-start(f32[8]{0:T(128)} %param.29) | copy-start | bytes 100
  77.4 13.2 %all-to-all-start.4 = ((bf16[8,64,512]{2,1,0:T(8,128)(2,1)}), bf16[8,64,512]{2,1,0:T(8,128)(2,1)S(1)}, u32[]{:S(2)}, u32[]{:S(2)}) async-start(bf16[8,64,512]{2,1,0:T(8,128)(2,1)} %broadcast_in_dim.10), calls=%async_computation.4 | async-start | bytes 1048576 | tf_op jit(solution)/shard_map/all_to_all | solution.py:143
  90.6 16.1 %all-to-all-start.5 = ((bf16[8,16,3072]{2,1,0:T(8,128)(2,1)}), bf16[8,16,3072]{2,1,0:T(8,128)(2,1)S(1)}, u32[]{:S(2)}, u32[]{:S(2)}) async-start(bf16[8,16,3072]{2,1,0:T(8,128)(2,1)} %bitcast.8), calls=%async_computation.5 | async-start | bytes 1572864 | tf_op jit(solution)/shard_map/all_to_all | solution.py:126
  94.1 156.6 %all-gather.4.cloned.1.call-start = ((), (), s32[]{:S(2)}) async-start(), calls=%async_computation.6 | async-start | bytes 3932160 | tf_op jit(solution)/shard_map/all_gather | solution.py:129
  106.6 0.9 copy-start.3
  110.1 1.6 copy-start.2
  187.3 2.8 %copy-start = (bf16[512,6144]{1,0:T(8,128)(2,1)S(1)}, bf16[512,6144]{1,0:T(8,128)(2,1)}, u32[]{:S(2)}) copy-start(bf16[512,6144]{1,0:T(8,128)(2,1)} %all-gather.6.cloned.1.call-done.piece_ref) | copy-start | bytes 18874372
  250.7 1.9 copy-start.1
Sparse Core Ops, SparseCore 0:
  25.2 46.4 all-gather.7
  73.3 113.9 all-gather.5
  188.9 61.7 all-gather.3

commit v2 on v1

--- a/solution.py
+++ b/solution.py
@@ -8,7 +8,7 @@
 from jax.sharding import PartitionSpec as P
 
 SLAB = 2048
-SHARES = (4, 12, 6)
+SHARES = (12, 10)
 
 
 ridge = 4.0
@@ -116,42 +116,48 @@
     tile, pieces = cuts(rows)
     split = design.reshape(rows_dev, row_count, rows)
 
+    first, width = pieces[0]
+    whole = lax.all_gather(split[:, :, first : first + width], "col", axis=0, tiled=True)
+
     gathered, token = [], None
-    ordered = None
-    for number, (first, width) in enumerate(pieces):
+    for first, width in pieces[1:]:
         source = split[:, :, first : first + width]
         if token is not None:
             source = after(source, token)
-        source = source.transpose(1, 0, 2)
-        own = lax.all_to_all(source, "row", split_axis=0, concat_axis=0, tiled=True)
+        own = lax.all_to_all(
+            source.transpose(1, 0, 2), "row", split_axis=0, concat_axis=0, tiled=True
+        )
         token = own
         gathered.append(
-            lax.all_gather(own.reshape(row_count * rows_dev, width), "col", axis=0, tiled=True)
+            lax.all_gather(own.reshape(row_count * rows_dev, -1), "col", axis=0, tiled=True)
         )
-        if number == 1:
-            slab_own = after(design[:, :SLAB], token)
-            columns = lax.all_to_all(slab_own, "col", split_axis=1, concat_axis=0, tiled=True)
-            facts = jnp.concatenate(
-                [arc_partials.reshape(1, -1), arc_id.astype(jnp.float32)[:, None]], axis=1
-            )
-            width_facts = facts.shape[1]
-            facts = jnp.broadcast_to(after(facts, columns), (devices, width_facts))
-            facts = lax.all_to_all(facts, ("row", "col"), split_axis=0, concat_axis=0, tiled=True)
-            spread = jnp.broadcast_to(
-                after(columns, facts)[None], (row_count,) + columns.shape
-            )
-            slab = lax.all_to_all(spread, "row", split_axis=0, concat_axis=0, tiled=True)
-            token = slab
-            slab = slab.reshape(epochs, columns.shape[1])
-            partials = facts[:, :-1].reshape(devices, order, rows_dev)
-            ids = facts[:, -1].astype(jnp.int32)
-            eliminated = eliminated_columns(slab, partials, ids, arc_weight)
-            ordered = eliminated.reshape(row_count, col_count, rows_dev, -1)
-            ordered = ordered.transpose(1, 0, 2, 3).reshape(epochs, -1)
 
-    total = None
-    for (first, width), piece in zip(pieces, gathered):
-        total = product_into(total, piece, ordered, first, tile, rows, 1.0 / epochs)
+    slab_own = design[:, :SLAB]
+    if token is not None:
+        slab_own = after(slab_own, token)
+    columns = lax.all_to_all(slab_own, "col", split_axis=1, concat_axis=0, tiled=True)
+    facts = jnp.concatenate(
+        [arc_partials.reshape(1, -1), arc_id.astype(jnp.float32)[:, None]], axis=1
+    )
+    facts = jnp.broadcast_to(after(facts, columns), (devices, facts.shape[1]))
+    facts = lax.all_to_all(facts, ("row", "col"), split_axis=0, concat_axis=0, tiled=True)
+    spread = jnp.broadcast_to(after(columns, facts)[None], (row_count,) + columns.shape)
+    slab = lax.all_to_all(spread, "row", split_axis=0, concat_axis=0, tiled=True)
+    partials = facts[:, :-1].reshape(devices, order, rows_dev)
+    ids = facts[:, -1].astype(jnp.int32)
+    eliminated = eliminated_columns(slab.reshape(epochs, -1), partials, ids, arc_weight)
+    ordered = eliminated.reshape(row_count, col_count, rows_dev, -1)
+    ordered = ordered.transpose(1, 0, 2, 3).reshape(epochs, -1)
+
+    dealt = lax.all_to_all(
+        after(whole, eliminated).transpose(1, 0, 2), "row", split_axis=0, concat_axis=0, tiled=True
+    )
+    scale = 1.0 / epochs
+    total = product_into(
+        None, dealt.reshape(epochs, -1), eliminated, pieces[0][0], tile, rows, scale
+    )
+    for (first, width), piece in zip(pieces[1:], gathered):
+        total = product_into(total, piece, ordered, first, tile, rows, scale)
     return total
 
 

time: 265 us -> 248 us (0.936)
  blocking collectives: 38.9 us -> 0 us
  waiting for transfers between devices: 157 us -> 172 us
  starting transfers between devices: 14.6 us -> 21.4 us
  local copies, waits for them, and re-layouts: 17.6 us -> 14.2 us
  Pallas kernels: 17.9 us -> 20.6 us
    all_to_all x1 -> x2, waiting for transfers between devices: 11.5 us -> 88.1 us  [the longest x1 71.5 us: local(): lax.all_to_all(after(whole, eliminated).transpose(1, 0, 2), 'row', split_...]
    all_gather x3 -> x2, waiting for transfers between devices: 123 us -> 59.3 us  [the longest x1 50.5 us: local(): lax.all_gather(split[:, :, first:first + width], 'col', axis=0, tiled=True)]
    all_to_all x2 -> x0, blocking collectives: 38.9 us -> none  [local(): own = lax.all_to_all(source, 'row', split_axis=0, concat_axis=0, tiled=True)]
    all_to_all x1 -> x2, starting transfers between devices: 3.55 us -> 10.1 us  [the longest x1 5.33 us: local(): lax.all_to_all(source.transpose(1, 0, 2), 'row', split_axis=0, concat_axi...]
    pallas_call x3 -> x2, Pallas kernels: 17.9 us -> 20.6 us  [product_into(): pl.pallas_call(functools.partial(product_kernel, scale), out_shape=jax.Sh...]
    unnamed x14 -> x11, local copies, waits for them, and re-layouts: 10.8 us -> 9.7 us
  transfers between devices with their start and end apart: 7 -> 7, of which waited for: 6 -> 7; matrix products, arithmetic and copies ran while one was open for 4% -> 4% of each run, Pallas kernels for 5% -> 5%
where the time goes in v2:
time: 248 us; the launch traced here: 247 us
  waiting for transfers between devices  172 us (69%)
  starting transfers between devices  21.4 us (9%)
  Pallas kernels  20.6 us (8%)
  between operations  14.5 us (6%)
  local copies, waits for them, and re-layouts  14.2 us (6%)
    all_to_all x1, waiting for transfers between devices, local(): lax.all_to_all(after(whole, eliminated).transpose(1, 0, 2), 'row', split_...  71.5 us
    all_gather x1, waiting for transfers between devices, local(): lax.all_gather(split[:, :, first:first + width], 'col', axis=0, tiled=True)  50.5 us
    pallas_call x2, Pallas kernels, product_into(): pl.pallas_call(functools.partial(product_kernel, scale), out_shape=jax.Sh...  20.6 us
    all_to_all x1, waiting for transfers between devices, local(): lax.all_to_all(source.transpose(1, 0, 2), 'row', split_axis=0, concat_axi...  16.6 us
    unnamed x11, local copies, waits for them, and re-layouts  9.7 us
    all_to_all x1, waiting for transfers between devices, local(): lax.all_to_all(spread, 'row', split_axis=0, concat_axis=0, tiled=True)  9.08 us
    all_gather x1, waiting for transfers between devices, local(): lax.all_gather(own.reshape(row_count * rows_dev, -1), 'col', axis=0, tile...  8.79 us
    all_to_all x1, waiting for transfers between devices, local(): lax.all_to_all(slab_own, 'col', split_axis=1, concat_axis=0, tiled=True)  8.51 us
  transfers between devices with their start and end apart: 7, of which 7 were waited for; matrix products, arithmetic and copies ran while one was open for 4% of the time, Pallas kernels for 5%

profile of v2, /device:TPU:0, one launch (start us, length us, event | category | flops | bytes accessed | tf_op | source)
XLA Modules:
  0.0 247.0 jit_solution(3626468551641029640)
XLA Ops:
  6.5 3.4 %copy.162 = bf16[2,8,8,11264]{3,2,1,0:T(8,128)(2,1)S(1)} copy(bf16[2,8,8,11264]{3,1,2,0:T(8,128)(2,1)} %bitcast.111) | data formatting | bytes 5767168
  10.0 2.0 copy.160
  12.2 1.8 copy.173
  14.0 5.3 %all-to-all-start = ((bf16[8,16,5120]{2,1,0:T(8,128)(2,1)}), bf16[8,16,5120]{2,1,0:T(8,128)(2,1)S(1)}, u32[]{:S(2)}, u32[]{:S(2)}) async-start(bf16[8,16,5120]{2,1,0:T(8,128)(2,1)} %bitcast.95), calls=%async_computation | async-start | bytes 2621440 | tf_op jit(solution)/shard_map/all_to_all | solution.py:127
  19.3 0.8 slice.305
  20.9 16.6 %all-to-all-done = bf16[8,16,5120]{2,1,0:T(8,128)(2,1)S(1)} async-done(((bf16[8,16,5120]{2,1,0:T(8,128)(2,1)}), bf16[8,16,5120]{2,1,0:T(8,128)(2,1)S(1)}, u32[]{:S(2)}, u32[]{:S(2)}) %all-to-all-start) | async-done | bytes 1310752 | tf_op jit(solution)/shard_map/all_to_all | solution.py:127
  37.5 0.7 copy.174
  38.2 4.9 %all-to-all-start.1 = ((bf16[16,4,512]{2,0,1:T(8,128)(2,1)}), bf16[16,4,512]{2,0,1:T(8,128)(2,1)S(1)}, u32[]{:S(2)}, u32[]{:S(2)}) async-start(bf16[16,4,512]{2,0,1:T(8,128)(2,1)} %bitcast.96), calls=%async_computation.1 | async-start | bytes 131072 | tf_op jit(solution)/shard_map/all_to_all | solution.py:138
  43.1 8.5 %all-to-all-done.1 = bf16[16,4,512]{2,0,1:T(8,128)(2,1)S(1)} async-done(((bf16[16,4,512]{2,0,1:T(8,128)(2,1)}), bf16[16,4,512]{2,0,1:T(8,128)(2,1)S(1)}, u32[]{:S(2)}, u32[]{:S(2)}) %all-to-all-start.1) | async-done | bytes 65568 | tf_op jit(solution)/shard_map/all_to_all | solution.py:138
  51.6 0.6 broadcast_in_dim.9
  52.2 2.9 %all-to-all-start.2 = ((f32[32,1,97]{2,1,0:T(1,128)}), f32[32,1,97]{2,1,0:T(1,128)S(1)}, u32[]{:S(2)}, u32[]{:S(2)}) async-start(f32[32,1,97]{2,1,0:T(1,128)} %broadcast_in_dim.9), calls=%async_computation.2 | async-start | bytes 32768 | tf_op jit(solution)/shard_map/all_to_all | solution.py:143
  55.2 0.7 all-gather.3.cloned.1.call-update
  55.9 6.8 %all-to-all-done.2 = f32[32,1,97]{2,1,0:T(1,128)S(1)} async-done(((f32[32,1,97]{2,1,0:T(1,128)}), f32[32,1,97]{2,1,0:T(1,128)S(1)}, u32[]{:S(2)}, u32[]{:S(2)}) %all-to-all-start.2) | async-done | bytes 12448 | tf_op jit(solution)/shard_map/all_to_all | solution.py:143
  62.8 0.1 copy.110
  62.9 0.4 fusion.41
  63.3 0.2 convolution_add_fusion
  64.2 0.1 mul.360
  64.4 0.1 mul.358
  64.6 0.8 broadcast_in_dim.11
  65.4 3.5 %all-to-all-start.3 = ((bf16[8,64,512]{2,1,0:T(8,128)(2,1)}), bf16[8,64,512]{2,1,0:T(8,128)(2,1)S(1)}, u32[]{:S(2)}, u32[]{:S(2)}) async-start(bf16[8,64,512]{2,1,0:T(8,128)(2,1)} %broadcast_in_dim.11), calls=%async_computation.3 | async-start | bytes 1048576 | tf_op jit(solution)/shard_map/all_to_all | solution.py:145
  68.9 0.2 broadcast_multiply_fusion
  69.1 0.4 mul.356
  69.5 9.1 %all-to-all-done.3 = bf16[8,64,512]{2,1,0:T(8,128)(2,1)S(1)} async-done(((bf16[8,64,512]{2,1,0:T(8,128)(2,1)}), bf16[8,64,512]{2,1,0:T(8,128)(2,1)S(1)}, u32[]{:S(2)}, u32[]{:S(2)}) %all-to-all-start.3) | async-done | bytes 524320 | tf_op jit(solution)/shard_map/all_to_all | solution.py:145
  78.6 0.4 fusion.3
  80.4 1.1 fusion.1.slab_ref
  81.5 50.5 %all-gather.5.cloned.1.call-done = bf16[64,8,6144]{2,0,1:T(8,128)(2,1)} async-done(((bf16[16,8,6144]{2,0,1:T(8,128)(2,1)}), bf16[64,8,6144]{2,0,1:T(8,128)(2,1)}) %all-gather.5.cloned.1.call-update) | async-done | bytes 6291472 | tf_op jit(solution)/shard_map/all_gather | solution.py:120
  132.0 4.8 %all-to-all-start.4 = ((bf16[8,64,6144]{2,1,0:T(8,128)(2,1)}), bf16[8,64,6144]{2,1,0:T(8,128)(2,1)}, u32[]{:S(2)}, u32[]{:S(2)}) async-start(bf16[8,64,6144]{2,1,0:T(8,128)(2,1)} %bitcast.107), calls=%async_computation.4 | async-start | bytes 12582912 | tf_op jit(solution)/shard_map/all_to_all | solution.py:152
  136.8 71.5 %all-to-all-done.4 = bf16[8,64,6144]{2,1,0:T(8,128)(2,1)} async-done(((bf16[8,64,6144]{2,1,0:T(8,128)(2,1)}), bf16[8,64,6144]{2,1,0:T(8,128)(2,1)}, u32[]{:S(2)}, u32[]{:S(2)}) %all-to-all-start.4) | async-done | bytes 6291488 | tf_op jit(solution)/shard_map/all_to_all | solution.py:152
  208.3 12.7 %shard_map.46.rest_0_ = f32[11264,512]{1,0:T(8,128)} custom-call(bf16[512,6144]{1,0:T(8,128)(2,1)} %bitcast.53.piece_ref, bf16[512,512]{1,0:T(8,128)(2,1)S(1)} %fusion.1.slab_ref), custom_call_target="tpu_custom_call" | custom-call | flops 3221225472 | bytes 19398656 | tf_op jit(solution)/shard_map/pallas_call | solution.py:82
  221.0 8.8 %all-gather.3.cloned.1.call-done.piece_ref = bf16[512,5120]{1,0:T(8,128)(2,1)} async-done(((bf16[128,5120]{1,0:T(8,128)(2,1)}), bf16[512,5120]{1,0:T(8,128)(2,1)}) %all-gather.3.cloned.1.call-update) | async-done | bytes 5242896 | tf_op jit(solution)/shard_map/all_gather | solution.py:132
  229.8 2.5 %copy-done = bf16[512,5120]{1,0:T(8,128)(2,1)S(1)} copy-done((bf16[512,5120]{1,0:T(8,128)(2,1)S(1)}, bf16[512,5120]{1,0:T(8,128)(2,1)}, u32[]{:S(2)}) %copy-start) | copy-done | bytes 5242904
  232.3 7.9 %shard_map.47 = f32[11264,512]{1,0:T(8,128)} custom-call(bf16[512,5120]{1,0:T(8,128)(2,1)S(1)} %copy-done, bf16[512,512]{1,0:T(8,128)(2,1)S(1)} %bitcast.104, f32[11264,512]{1,0:T(8,128)} %shard_map.46.rest_0_), custom_call_target="tpu_custom_call", output_to_operand_aliasing={{}: (2, {})} | custom-call | flops 2684354560 | bytes 16252928 | tf_op jit(solution)/shard_map/pallas_call | solution.py:82
  (79 shorter events, 2.6 us)
Async XLA Ops:
  6.5 125.4 %all-gather.5.cloned.1.call-start = ((), (), s32[]{:S(2)}) async-start(), calls=%async_computation.6 | async-start | bytes 7864320 | tf_op jit(solution)/shard_map/all_gather | solution.py:120
  12.2 8.6 %copy-start.2 = (f32[1,6,16]{2,0,1:T(1,128)S(1)}, f32[1,6,16]{2,0,1:T(1,128)}, u32[]{:S(2)}) copy-start(f32[1,6,16]{2,0,1:T(1,128)} %param.27) | copy-start | bytes 1156
  14.0 49.9 %copy-start.3 = (f32[8]{0:T(128)S(1)}, f32[8]{0:T(128)}, u32[]{:S(2)}) copy-start(f32[8]{0:T(128)} %param.29) | copy-start | bytes 100
  14.0 23.5 %all-to-all-start = ((bf16[8,16,5120]{2,1,0:T(8,128)(2,1)}), bf16[8,16,5120]{2,1,0:T(8,128)(2,1)S(1)}, u32[]{:S(2)}, u32[]{:S(2)}) async-start(bf16[8,16,5120]{2,1,0:T(8,128)(2,1)} %bitcast.95), calls=%async_computation | async-start | bytes 2621440 | tf_op jit(solution)/shard_map/all_to_all | solution.py:127
  37.5 17.7 %copy-start.1 = (bf16[8,16,5120]{2,1,0:T(8,128)(2,1)}, bf16[8,16,5120]{2,1,0:T(8,128)(2,1)S(1)}, u32[]{:S(2)}) copy-start(bf16[8,16,5120]{2,1,0:T(8,128)(2,1)S(1)} %all-to-all-done) | copy-start | bytes 3932164
  38.2 13.5 %all-to-all-start.1 = ((bf16[16,4,512]{2,0,1:T(8,128)(2,1)}), bf16[16,4,512]{2,0,1:T(8,128)(2,1)S(1)}, u32[]{:S(2)}, u32[]{:S(2)}) async-start(bf16[16,4,512]{2,0,1:T(8,128)(2,1)} %bitcast.96), calls=%async_computation.1 | async-start | bytes 131072 | tf_op jit(solution)/shard_map/all_to_all | solution.py:138
  52.2 10.4 %all-to-all-start.2 = ((f32[32,1,97]{2,1,0:T(1,128)}), f32[32,1,97]{2,1,0:T(1,128)S(1)}, u32[]{:S(2)}, u32[]{:S(2)}) async-start(f32[32,1,97]{2,1,0:T(1,128)} %broadcast_in_dim.9), calls=%async_computation.2 | async-start | bytes 32768 | tf_op jit(solution)/shard_map/all_to_all | solution.py:143
  55.1 174.6 %all-gather.3.cloned.1.call-start = ((), (), s32[]{:S(2)}) async-start(), calls=%async_computation.5 | async-start | bytes 6553600 | tf_op jit(solution)/shard_map/all_gather | solution.py:132
  65.4 13.1 %all-to-all-start.3 = ((bf16[8,64,512]{2,1,0:T(8,128)(2,1)}), bf16[8,64,512]{2,1,0:T(8,128)(2,1)S(1)}, u32[]{:S(2)}, u32[]{:S(2)}) async-start(bf16[8,64,512]{2,1,0:T(8,128)(2,1)} %broadcast_in_dim.11), calls=%async_computation.3 | async-start | bytes 1048576 | tf_op jit(solution)/shard_map/all_to_all | solution.py:145
  132.0 76.3 %all-to-all-start.4 = ((bf16[8,64,6144]{2,1,0:T(8,128)(2,1)}), bf16[8,64,6144]{2,1,0:T(8,128)(2,1)}, u32[]{:S(2)}, u32[]{:S(2)}) async-start(bf16[8,64,6144]{2,1,0:T(8,128)(2,1)} %bitcast.107), calls=%async_computation.4 | async-start | bytes 12582912 | tf_op jit(solution)/shard_map/all_to_all | solution.py:152
  229.8 2.5 %copy-start = (bf16[512,5120]{1,0:T(8,128)(2,1)S(1)}, bf16[512,5120]{1,0:T(8,128)(2,1)}, u32[]{:S(2)}) copy-start(bf16[512,5120]{1,0:T(8,128)(2,1)} %all-gather.3.cloned.1.call-done.piece_ref) | copy-start | bytes 15728644
Sparse Core Ops, SparseCore 0:
  12.2 119.7 all-gather.4
  133.5 96.1 all-gather.2
